TPU v7x, 256 devices: a whole 4x4x8 slice. The times are simulated.
256 devices in a mesh: row: 32 (over z, y_lo, core), col: 8 (over y_hi, x).
Axes of the slice: x: 4, y: 4 (y_hi: 2, y_lo: 2; y = y_hi * 2 + y_lo), z: 8, core: 2. Of those that a mesh axis runs over, the one named last changes fastest.
Arguments:
- queries: bfloat16 [256, 256, 2240], P('row', 'col'), may hold values from -6 to 6
- keys: bfloat16 [256, 256, 2240], P('row', 'col'), may hold values from -120 to 120
- values: bfloat16 [256, 256, 2240], P('row', 'col'), may hold values from -10 to 10
- features: bfloat16 [256, 256, 11200], P('row', 'col'), may hold values from -6 to 6
- conv_weight: bfloat16 [3, 3, 11200], replicated, may hold values from -2 to 2
- conv_bias: bfloat16 [11200], replicated, may hold values from -3 to 3
Outputs:
- attended: bfloat16 [256, 256, 2240], P('row', 'col')
- gated: bfloat16 [256, 256, 5600], P('row', 'col')
All inputs are finite; a program needn't handle non-finite values.
Results may differ from a plain program's by a relative error of at most 0.001.
Values may be sent and summed in bfloat16 or wider, within the bound.
A program may use at most 128 MiB of HBM per device.

v0:
```python
import jax
import jax.numpy as jnp
from jax import lax
from jax.sharding import PartitionSpec as P

HEADS = 70
HEAD_DIM = 32
HID = 5600


def padded_2(block, sides, width):
    for axis, dim in sides:
        count = lax.axis_size(axis)
        forward = [(i, i + 1) for i in range(count - 1)]
        backward = [(target, source) for source, target in forward]
        low = lax.ppermute(
            lax.slice_in_dim(block, block.shape[dim] - width, None, axis=dim), axis, forward
        )
        high = lax.ppermute(lax.slice_in_dim(block, 0, width, axis=dim), axis, backward)
        block = jnp.concatenate([low, block, high], axis=dim)
    return block


def on_device(queries, keys, values, features, conv_weight, conv_bias):
    tile_rows, tile_cols, channels = queries.shape
    key_heads = jnp.maximum(keys.reshape(-1, HEADS, HEAD_DIM), 0)
    value_heads = values.reshape(-1, HEADS, HEAD_DIM)
    local_state = jnp.einsum(
        "thj,thi->jhi", value_heads, key_heads, preferred_element_type=jnp.float32
    ).reshape(HEAD_DIM, channels)
    local_keys = jnp.sum(key_heads, axis=0, dtype=jnp.float32).reshape(1, channels)
    state_sum, key_sum = lax.psum((local_state, local_keys), ("row", "col"))
    kv_state = state_sum.reshape(HEAD_DIM, HEADS, HEAD_DIM)
    key_total = key_sum.reshape(HEADS, HEAD_DIM)
    query_heads = jnp.maximum(queries.reshape(-1, HEADS, HEAD_DIM), 0).astype(jnp.float32)
    numerator = jnp.einsum("thi,jhi->thj", query_heads, kv_state, precision=lax.Precision.HIGHEST)
    denominator = jnp.einsum("thi,hi->th", query_heads, key_total, precision=lax.Precision.HIGHEST)
    attended = (
        (numerator / (denominator[:, :, None] + 1e-15))
        .astype(jnp.bfloat16)
        .reshape(tile_rows, tile_cols, channels)
    )
    padded = padded_2(features, (("row", 0), ("col", 1)), 1)
    weight_float = conv_weight.astype(jnp.float32)
    conv_sum = conv_bias.astype(jnp.float32)
    for tap_row in range(3):
        for tap_col in range(3):
            window = padded[tap_row : tap_row + tile_rows, tap_col : tap_col + tile_cols]
            conv_sum = conv_sum + weight_float[tap_row, tap_col] * window.astype(jnp.float32)
    gated = (conv_sum[:, :, :HID] * jax.nn.silu(conv_sum[:, :, HID:])).astype(jnp.bfloat16)
    return (attended, gated)


def solution(mesh):
    return jax.shard_map(
        on_device,
        mesh=mesh,
        in_specs=(
            P("row", "col", None),
            P("row", "col", None),
            P("row", "col", None),
            P("row", "col", None),
            P(),
            P(),
        ),
        out_specs=(P("row", "col", None), P("row", "col", None)),
        check_vma=False,
    )
```

profile of v0, /device:TPU:6, one launch (start us, length us, event | category | flops | bytes accessed | tf_op | source)
XLA Modules:
  0.0 376.9 jit_solution(7483596677770068258)
XLA Ops:
  7.2 2.4 fusion.13
  9.6 2.6 collective-permute-start
  12.2 1.3 collective-permute-start.1
  13.5 1.4 broadcast_maximum_fusion.1
  14.8 5.0 %reshape.43 = bf16[256,70,32]{2,1,0:T(8,128)(2,1)} reshape(bf16[8,32,2240]{2,1,0:T(8,128)(2,1)S(1)} %broadcast_maximum_fusion.1) | data formatting | bytes 2293760 | tf_op jit(solution)/shard_map/max | solution.py:26
  19.9 4.9 %reshape.44 = bf16[256,70,32]{2,1,0:T(8,128)(2,1)} reshape(bf16[8,32,2240]{2,1,0:T(8,128)(2,1)S(1)} %copy-done.6) | data formatting | bytes 2293760 | tf_op jit(solution)/shard_map/reshape | solution.py:27
  24.8 6.3 %fusion.5 = f32[32,70,32]{0,2,1:T(8,128)} fusion(bf16[256,70,32]{2,1,0:T(8,128)(2,1)} %reshape.44, bf16[256,70,32]{2,1,0:T(8,128)(2,1)} %reshape.43), kind=kOutput, calls=%fused_computation.13 | convolution fusion | flops 36700160 | bytes 2580480 | tf_op jit(solution)/shard_map/thj,thi->jhi/dot_general | solution.py:28
  32.2 8.3 %copy.31 = bf16[8,32,11200]{2,0,1:T(8,128)(2,1)} copy(bf16[8,32,11200]{2,1,0:T(8,128)(2,1)} %param.9) | data formatting | bytes 11468800 | tf_op args[3]
  40.5 4.9 %reshape.45 = bf16[256,70,32]{2,1,0:T(8,128)(2,1)} reshape(bf16[8,32,2240]{2,1,0:T(8,128)(2,1)S(1)} %broadcast_maximum_fusion) | data formatting | bytes 2293760 | tf_op jit(solution)/shard_map/max | solution.py:35
  45.4 6.1 %copy.45 = bf16[256,70,32]{0,2,1:T(8,128)(2,1)S(1)} copy(bf16[256,70,32]{2,1,0:T(8,128)(2,1)} %reshape.45) | data formatting | bytes 2293760 | tf_op jit(solution)/shard_map/max | solution.py:35
  51.9 81.2 %psum.15 = f32[70,32]{1,0:T(8,128)S(1)} all-reduce(f32[70,32]{1,0:T(8,128)S(1)} %reshape.37), channel_id=1, replica_groups=mesh['row'=32,'col'=8] {'row','col'}, use_global_device_ids=true, to_apply=%region_2.0 | all-reduce | flops 2240 | bytes 17920 | tf_op jit(solution)/shard_map/psum | solution.py:32
  134.3 2.2 copy.30
  136.6 2.3 copy.32
  140.0 2.1 pad_maximum_fusion.5
  142.1 5.5 %collective-permute-start.2 = (bf16[10,1,11200]{2,0,1:T(8,128)(2,1)}, bf16[10,1,11200]{2,0,1:T(8,128)(2,1)}, u32[]{:S(2)}, u32[]{:S(2)}) collective-permute-start(bf16[10,1,11200]{2,0,1:T(8,128)(2,1)} %get-tuple-element.12), channel_id=1, source_target_pairs={{0,1},{1,2},{2,3},{3,4},{4,5},{5,6},{6,7},{8,9},{9,10},{10,11},{11... | collective-permute-start | bytes 672008 | tf_op jit(solution)/shard_map/ppermute | solution.py:16
  147.6 1.9 collective-permute-start.3
  149.6 145.6 %all-reduce.2.cloned.1.call-done = f32[32,70,32]{0,2,1:T(8,128)} async-done(((f32[32,70,32]{0,2,1:T(8,128)}), f32[32,70,32]{0,2,1:T(8,128)}) %all-reduce.2.cloned.1.call-update) | async-done | bytes 286736 | tf_op jit(solution)/shard_map/psum | solution.py:32
  295.2 3.4 fusion.4
  298.6 6.0 %reshape.38 = bf16[8,32,2240]{1,0,2:T(8,128)(2,1)} reshape(bf16[256,70,32]{0,2,1:T(8,128)(2,1)} %fusion.4) | data formatting | bytes 2293760 | tf_op jit(solution)/shard_map/reshape | solution.py:41
  304.7 6.3 %copy.38 = bf16[8,32,2240]{2,1,0:T(8,128)(2,1)} copy(bf16[8,32,2240]{1,0,2:T(8,128)(2,1)} %reshape.38) | data formatting | bytes 2293760
  311.1 22.1 %maximum_maximum_fusion = (bf16[10,33,11200]{2,0,1:T(8,128)(2,1)}, bf16[10,33,11200]{2,0,1:T(8,128)(2,1)}) fusion(bf16[1,32,11200]{2,0,1:T(2,128)(2,1)} %copy-done, bf16[8,32,11200]{2,0,1:T(8,128)(2,1)} %copy.31, bf16[1,32,11200]{2,0,1:T(2,128)(2,1)S(1)} %copy.30, bf16[10,1,11200]{2,0,1:T(8,128)(2,1)} %collective-permute-done.2, ...), kind=kLoop, calls=%fused_computation | loop fusion | flops 59136000 | bytes 22400000 | tf_op jit(solution)/shard_map/concatenate | solution.py:20
  333.3 29.1 %multiply_add_fusion = f32[8,32,11200]{2,0,1:T(8,128)} fusion(bf16[8,32,11200]{2,0,1:T(8,128)(2,1)S(1)} %bitcast.28, bf16[10,33,11200]{2,0,1:T(8,128)(2,1)} %get-tuple-element.11, bf16[1,32,11200]{2,0,1:T(2,128)(2,1)S(1)} %copy-done.1, bf16[10,33,11200]{2,0,1:T(8,128)(2,1)} %get-tuple-element.10, bf16[1,32,11200]{2,0,1:T(2,128)(2,1)S(1)} %copy.30, ...), kind=kLoop, calls=%fused_computation.2 | loop fusion | flops 94617600 | bytes 53491200 | tf_op jit(solution)/shard_map/add | solution.py:49
  362.4 5.2 %fusion = bf16[8,32,5600]{2,0,1:T(8,128)(2,1)S(1)} fusion(f32[8,32,11200]{2,0,1:T(8,128)} %multiply_add_fusion), kind=kLoop, calls=%fused_computation.4 | loop fusion | flops 8601600 | bytes 14336000 | tf_op jit(solution)/shard_map/convert_element_type | solution.py:50
  367.7 2.4 copy.39
  (50 shorter events, 3.8 us)
Async XLA Ops:
  7.2 12.7 %copy-start.6 = (bf16[8,32,2240]{2,1,0:T(8,128)(2,1)S(1)}, bf16[8,32,2240]{2,1,0:T(8,128)(2,1)}, u32[]{:S(2)}) copy-start(bf16[8,32,2240]{2,1,0:T(8,128)(2,1)} %param.8) | copy-start | bytes 3440644
  7.2 288.0 %all-reduce.2.cloned.1.call-start = ((), (), s32[]{:S(2)}) async-start(), calls=%async_computation | async-start | bytes 2293760 | tf_op jit(solution)/shard_map/psum | solution.py:32
  9.6 124.7 %collective-permute-start = (bf16[1,32,11200]{2,1,0:T(8,128)(2,1)S(1)}, bf16[1,32,11200]{2,1,0:T(8,128)(2,1)}, u32[]{:S(2)}, u32[]{:S(2)}) collective-permute-start(bf16[1,32,11200]{2,1,0:T(8,128)(2,1)S(1)} %get-tuple-element.14), channel_id=1, source_target_pairs={{0,8},{8,16},{16,24},{24,32},{32,40},{40,48},{48,56},{56,64},{64,7... | collective-permute-start | bytes 2150408 | tf_op jit(solution)/shard_map/ppermute | solution.py:16
  12.2 124.4 %collective-permute-start.1 = (bf16[1,32,11200]{2,1,0:T(8,128)(2,1)}, bf16[1,32,11200]{2,1,0:T(8,128)(2,1)}, u32[]{:S(2)}, u32[]{:S(2)}) collective-permute-start(bf16[1,32,11200]{2,1,0:T(8,128)(2,1)} %get-tuple-element.15), channel_id=1, source_target_pairs={{8,0},{16,8},{24,16},{32,24},{40,32},{48,40},{56,48},{64,56},{72,6... | collective-permute-start | bytes 2150408 | tf_op jit(solution)/shard_map/ppermute | solution.py:19
  24.8 6.4 %copy-start.7 = (bf16[3,3,11200]{2,1,0:T(4,128)(2,1)S(1)}, bf16[3,3,11200]{2,1,0:T(4,128)(2,1)}, u32[]{:S(2)}) copy-start(bf16[3,3,11200]{2,1,0:T(4,128)(2,1)} %param.10) | copy-start | bytes 604804
  24.8 7.3 %copy-start.5 = (bf16[8,32,2240]{2,1,0:T(8,128)(2,1)S(1)}, bf16[8,32,2240]{2,1,0:T(8,128)(2,1)}, u32[]{:S(2)}) copy-start(bf16[8,32,2240]{2,1,0:T(8,128)(2,1)} %param.6) | copy-start | bytes 3440644
  32.2 8.3 %copy-start.15 = (bf16[11200]{0:T(1024)(128)(2,1)S(1)}, bf16[11200]{0:T(1024)(128)(2,1)}, u32[]{:S(2)}) copy-start(bf16[11200]{0:T(1024)(128)(2,1)} %param.11) | copy-start | bytes 67204
  40.5 11.0 %copy-start.2 = (bf16[8,32,2240]{2,1,0:T(8,128)(2,1)S(1)}, bf16[8,32,2240]{2,1,0:T(8,128)(2,1)}, u32[]{:S(2)}) copy-start(bf16[8,32,2240]{2,1,0:T(8,128)(2,1)} %param.7) | copy-start | bytes 3440644
  51.5 82.8 %copy-start.3 = (bf16[256,70,32]{0,2,1:T(8,128)(2,1)}, bf16[256,70,32]{0,2,1:T(8,128)(2,1)S(1)}, u32[]{:S(2)}) copy-start(bf16[256,70,32]{0,2,1:T(8,128)(2,1)S(1)} %copy.45) | copy-start | bytes 3440644
  136.5 158.7 %copy-start.4 = (bf16[256,70,32]{0,2,1:T(8,128)(2,1)S(1)}, bf16[256,70,32]{0,2,1:T(8,128)(2,1)}, u32[]{:S(2)}) copy-start(bf16[256,70,32]{0,2,1:T(8,128)(2,1)} %copy-done.3) | copy-start | bytes 3440644
  136.5 158.7 %copy-start.14 = (f32[256,70]{0,1:T(8,128)S(1)}, f32[256,70]{0,1:T(8,128)}, u32[]{:S(2)}) copy-start(f32[256,70]{0,1:T(8,128)} %fusion.10) | copy-start | bytes 215044
  138.9 1.1 copy-start
  142.1 169.0 %collective-permute-start.2 = (bf16[10,1,11200]{2,0,1:T(8,128)(2,1)}, bf16[10,1,11200]{2,0,1:T(8,128)(2,1)}, u32[]{:S(2)}, u32[]{:S(2)}) collective-permute-start(bf16[10,1,11200]{2,0,1:T(8,128)(2,1)} %get-tuple-element.12), channel_id=1, source_target_pairs={{0,1},{1,2},{2,3},{3,4},{4,5},{5,6},{6,7},{8,9},{9,10},{10,11},{11... | collective-permute-start | bytes 672008 | tf_op jit(solution)/shard_map/ppermute | solution.py:16
  147.6 163.4 %collective-permute-start.3 = (bf16[10,1,11200]{2,0,1:T(8,128)(2,1)S(1)}, bf16[10,1,11200]{2,0,1:T(8,128)(2,1)}, u32[]{:S(2)}, u32[]{:S(2)}) collective-permute-start(bf16[10,1,11200]{2,0,1:T(8,128)(2,1)S(1)} %get-tuple-element.13), channel_id=1, source_target_pairs={{1,0},{2,1},{3,2},{4,3},{5,4},{6,5},{7,6},{9,8},{10,9},{11,10},{12... | collective-permute-start | bytes 672008 | tf_op jit(solution)/shard_map/ppermute | solution.py:19
  304.7 28.5 %slice-start = ((s8[5767168]{0:T(1024)(128)(4,1)}), s8[1572864]{0:T(1024)(128)(4,1)S(1)}, s32[]{:S(2)}) async-start(s8[5767168]{0:T(1024)(128)(4,1)} %bitcast.27), calls=%async_computation.1 | async-start | bytes 3145728
  311.0 22.2 %slice-start.1 = ((s8[5767168]{0:T(1024)(128)(4,1)}), s8[4194304]{0:T(1024)(128)(4,1)S(1)}, s32[]{:S(2)}) async-start(s8[5767168]{0:T(1024)(128)(4,1)} %bitcast.27), calls=%async_computation.2 | async-start | bytes 8388608
  311.0 22.2 %copy-start.1 = (bf16[1,32,11200]{2,0,1:T(2,128)(2,1)S(1)}, bf16[1,32,11200]{2,0,1:T(2,128)(2,1)}, u32[]{:S(2)}) copy-start(bf16[1,32,11200]{2,0,1:T(2,128)(2,1)} %copy-done) | copy-start | bytes 2150404
  311.0 22.2 %copy-start.8 = (f32[1,1,11200]{2,1,0:T(1,128)S(1)}, f32[1,1,11200]{2,1,0:T(1,128)}, u32[]{:S(2)}) copy-start(f32[1,1,11200]{2,1,0:T(1,128)} %get-tuple-element.19) | copy-start | bytes 134404
  311.0 22.2 %copy-start.9 = (f32[1,1,11200]{2,1,0:T(1,128)S(1)}, f32[1,1,11200]{2,1,0:T(1,128)}, u32[]{:S(2)}) copy-start(f32[1,1,11200]{2,1,0:T(1,128)} %get-tuple-element.20) | copy-start | bytes 134404
  311.0 22.2 %copy-start.10 = (f32[1,1,11200]{2,1,0:T(1,128)S(1)}, f32[1,1,11200]{2,1,0:T(1,128)}, u32[]{:S(2)}) copy-start(f32[1,1,11200]{2,1,0:T(1,128)} %get-tuple-element.21) | copy-start | bytes 134404
  311.0 22.2 %copy-start.11 = (f32[1,1,11200]{2,1,0:T(1,128)S(1)}, f32[1,1,11200]{2,1,0:T(1,128)}, u32[]{:S(2)}) copy-start(f32[1,1,11200]{2,1,0:T(1,128)} %get-tuple-element.22) | copy-start | bytes 134404
  311.0 22.2 %copy-start.12 = (f32[1,1,11200]{2,1,0:T(1,128)S(1)}, f32[1,1,11200]{2,1,0:T(1,128)}, u32[]{:S(2)}) copy-start(f32[1,1,11200]{2,1,0:T(1,128)} %get-tuple-element.23) | copy-start | bytes 134404
  311.0 22.2 %copy-start.13 = (f32[1,1,11200]{2,1,0:T(1,128)S(1)}, f32[1,1,11200]{2,1,0:T(1,128)}, u32[]{:S(2)}) copy-start(f32[1,1,11200]{2,1,0:T(1,128)} %get-tuple-element.24) | copy-start | bytes 134404
Sparse Core Ops, SparseCore 0:
  31.3 263.8 all-reduce.1
where the time goes:
time: 378 us; the launch traced here: 377 us
  waiting for transfers between devices  146 us (39%)
  blocking collectives  81.2 us (21%)
  other arithmetic  60.9 us (16%)
  local copies, waits for them, and re-layouts  53.1 us (14%)
  between operations  14.3 us (4%)
  starting transfers between devices  11.4 us (3%)
  matrix products  10.4 us (3%)
    psum x1, waiting for transfers between devices, on_device(): state_sum, key_sum = lax.psum((local_state, local_keys), ('row', 'col'))  146 us
    psum x1, blocking collectives, on_device(): state_sum, key_sum = lax.psum((local_state, local_keys), ('row', 'col'))  81.2 us
    add x1, other arithmetic, on_device(): conv_sum + weight_float[tap_row, tap_col] * window.astype(jnp.float32)  29.1 us
    concatenate x1, other arithmetic, padded_2(): block = jnp.concatenate([low, block, high], axis=dim)  22.1 us
    unnamed x39, local copies, waits for them, and re-layouts  18.2 us
    max x2, local copies, waits for them, and re-layouts, on_device(): jnp.maximum(queries.reshape(-1, HEADS, HEAD_DIM), 0).astype(jnp.float32)  11 us
    ppermute x2, starting transfers between devices, padded_2(): lax.ppermute(lax.slice_in_dim(block, block.shape[dim] - width, None, axis...  8.14 us
  transfers between devices with their start and end apart: 5, of which 1 were waited for; matrix products, arithmetic and copies ran while one was open for 16% of the time, Pallas kernels for 0%

commit v1 on v0

--- a/solution.py
+++ b/solution.py
@@ -29,7 +29,8 @@
         "thj,thi->jhi", value_heads, key_heads, preferred_element_type=jnp.float32
     ).reshape(HEAD_DIM, channels)
     local_keys = jnp.sum(key_heads, axis=0, dtype=jnp.float32).reshape(1, channels)
-    state_sum, key_sum = lax.psum((local_state, local_keys), ("row", "col"))
+    save_cells = lambda x_in: lax.psum(lax.psum(x_in, "row"), "col")
+    state_sum, key_sum = save_cells((local_state, local_keys))
     kv_state = state_sum.reshape(HEAD_DIM, HEADS, HEAD_DIM)
     key_total = key_sum.reshape(HEADS, HEAD_DIM)
     query_heads = jnp.maximum(queries.reshape(-1, HEADS, HEAD_DIM), 0).astype(jnp.float32)

time: 378 us -> 424 us (1.12)
  waiting for transfers between devices: 146 us -> 170 us
  blocking collectives: 81.2 us -> 99.7 us
    psum x1 -> x2, waiting for transfers between devices: 146 us -> 170 us  [on_device(): save_cells = lambda x_in: lax.psum(lax.psum(x_in, 'row'), 'col')]
    psum x1 -> x2, blocking collectives: 81.2 us -> 99.7 us  [on_device(): save_cells = lambda x_in: lax.psum(lax.psum(x_in, 'row'), 'col')]
    unnamed x39 -> x37, local copies, waits for them, and re-layouts: 18.2 us -> 18.2 us
  transfers between devices with their start and end apart: 5 -> 6, of which waited for: 1 -> 2; matrix products, arithmetic and copies ran while one was open for 16% -> 15% of each run, Pallas kernels for 0% -> 0%
where the time goes in v1:
time: 424 us; the launch traced here: 422 us
  waiting for transfers between devices  170 us (40%)
  blocking collectives  99.7 us (24%)
  other arithmetic  60.2 us (14%)
  local copies, waits for them, and re-layouts  56.8 us (13%)
  between operations  14.4 us (3%)
  starting transfers between devices  10.8 us (3%)
  matrix products  9.28 us (2%)
    psum x2, waiting for transfers between devices, on_device(): save_cells = lambda x_in: lax.psum(lax.psum(x_in, 'row'), 'col')  170 us
    psum x2, blocking collectives, on_device(): save_cells = lambda x_in: lax.psum(lax.psum(x_in, 'row'), 'col')  99.7 us
    add x1, other arithmetic, on_device(): conv_sum + weight_float[tap_row, tap_col] * window.astype(jnp.float32)  29 us
    concatenate x1, other arithmetic, padded_2(): block = jnp.concatenate([low, block, high], axis=dim)  22.2 us
    unnamed x37, local copies, waits for them, and re-layouts  18.2 us
    max x2, local copies, waits for them, and re-layouts, on_device(): jnp.maximum(queries.reshape(-1, HEADS, HEAD_DIM), 0).astype(jnp.float32)  11 us
  transfers between devices with their start and end apart: 6, of which 2 were waited for; matrix products, arithmetic and copies ran while one was open for 15% of the time, Pallas kernels for 0%

profile of v1, /device:TPU:6, one launch (start us, length us, event | category | flops | bytes accessed | tf_op | source)
XLA Modules:
  0.0 421.6 jit_solution(331611903508125354)
XLA Ops:
  7.2 2.4 fusion.8
  9.6 2.6 collective-permute-start
  14.9 5.0 %reshape.41 = bf16[256,70,32]{2,1,0:T(8,128)(2,1)} reshape(bf16[8,32,2240]{2,1,0:T(8,128)(2,1)S(1)} %broadcast_maximum_fusion.1) | data formatting | bytes 2293760 | tf_op jit(solution)/shard_map/max | solution.py:26
  19.9 4.9 %reshape.42 = bf16[256,70,32]{2,1,0:T(8,128)(2,1)} reshape(bf16[8,32,2240]{2,1,0:T(8,128)(2,1)S(1)} %copy-done.6) | data formatting | bytes 2293760 | tf_op jit(solution)/shard_map/reshape | solution.py:27
  24.8 5.3 %fusion.1 = f32[70,32,32]{2,1,0:T(8,128)S(1)} fusion(bf16[256,70,32]{2,1,0:T(8,128)(2,1)} %reshape.42, bf16[256,70,32]{2,1,0:T(8,128)(2,1)} %reshape.41), kind=kOutput, calls=%fused_computation.7 | convolution fusion | flops 36700160 | bytes 2580480 | tf_op jit(solution)/shard_map/thj,thi->jhi/dot_general | solution.py:28
  32.4 5.0 %reshape.43 = bf16[256,70,32]{2,1,0:T(8,128)(2,1)} reshape(bf16[8,32,2240]{2,1,0:T(8,128)(2,1)S(1)} %broadcast_maximum_fusion) | data formatting | bytes 2293760 | tf_op jit(solution)/shard_map/max | solution.py:36
  37.3 6.1 %copy.50 = bf16[256,70,32]{0,2,1:T(8,128)(2,1)S(1)} copy(bf16[256,70,32]{2,1,0:T(8,128)(2,1)} %reshape.43) | data formatting | bytes 2293760 | tf_op jit(solution)/shard_map/max | solution.py:36
  43.7 63.0 %psum.30 = f32[1,2240]{1,0:T(1,128)S(1)} all-reduce(f32[1,2240]{1,0:T(1,128)S(1)} %reshape.36), channel_id=1, replica_groups=mesh['row'=32,'col'=8] {'row'}, use_global_device_ids=true, to_apply=%region_3.0 | all-reduce | flops 2240 | bytes 17920 | tf_op jit(solution)/shard_map/psum | solution.py:32
  106.8 36.7 %psum.31 = f32[70,32]{1,0:T(8,128)S(1)} all-reduce(f32[70,32]{1,0:T(8,128)S(1)} %reshape.37), channel_id=1, replica_groups=mesh['row'=32,'col'=8] {'col'}, use_global_device_ids=true, to_apply=%region_4.0 | all-reduce | flops 2240 | bytes 17920 | tf_op jit(solution)/shard_map/psum | solution.py:32
  144.1 8.3 %copy.37 = bf16[8,32,11200]{2,0,1:T(8,128)(2,1)} copy(bf16[8,32,11200]{2,1,0:T(8,128)(2,1)} %param.9) | data formatting | bytes 11468800 | tf_op args[3]
  152.4 91.5 %all-reduce.3.cloned.1.call-done = f32[32,2240]{1,0:T(8,128)} async-done(((f32[32,2240]{1,0:T(8,128)}), f32[32,2240]{1,0:T(8,128)}) %all-reduce.3.cloned.1.call-update) | async-done | bytes 286736 | tf_op jit(solution)/shard_map/psum | solution.py:32
  246.5 2.2 copy.36
  248.8 2.3 copy.38
  252.2 2.1 pad_maximum_fusion.5
  254.3 4.9 %collective-permute-start.2 = (bf16[10,1,11200]{2,0,1:T(8,128)(2,1)}, bf16[10,1,11200]{2,0,1:T(8,128)(2,1)}, u32[]{:S(2)}, u32[]{:S(2)}) collective-permute-start(bf16[10,1,11200]{2,0,1:T(8,128)(2,1)} %get-tuple-element.12), channel_id=1, source_target_pairs={{0,1},{1,2},{2,3},{3,4},{4,5},{5,6},{6,7},{8,9},{9,10},{10,11},{11... | collective-permute-start | bytes 672008 | tf_op jit(solution)/shard_map/ppermute | solution.py:16
  259.2 1.9 collective-permute-start.3
  261.1 79.0 %all-reduce.5.cloned.1.call-done = f32[32,70,32]{2,0,1:T(8,128)} async-done(((f32[32,70,32]{2,0,1:T(8,128)}), f32[32,70,32]{2,0,1:T(8,128)}) %all-reduce.5.cloned.1.call-update) | async-done | bytes 286736 | tf_op jit(solution)/shard_map/psum | solution.py:32
  340.1 3.4 fusion.4
  343.5 6.0 %reshape.38 = bf16[8,32,2240]{1,0,2:T(8,128)(2,1)} reshape(bf16[256,70,32]{0,2,1:T(8,128)(2,1)} %fusion.4) | data formatting | bytes 2293760 | tf_op jit(solution)/shard_map/reshape | solution.py:42
  349.5 6.3 %copy.44 = bf16[8,32,2240]{2,1,0:T(8,128)(2,1)} copy(bf16[8,32,2240]{1,0,2:T(8,128)(2,1)} %reshape.38) | data formatting | bytes 2293760
  355.9 22.2 %maximum_maximum_fusion = (bf16[10,33,11200]{2,0,1:T(8,128)(2,1)}, bf16[10,33,11200]{2,0,1:T(8,128)(2,1)}) fusion(bf16[1,32,11200]{2,0,1:T(2,128)(2,1)} %copy-done, bf16[8,32,11200]{2,0,1:T(8,128)(2,1)} %copy.37, bf16[1,32,11200]{2,0,1:T(2,128)(2,1)S(1)} %copy.36, bf16[10,1,11200]{2,0,1:T(8,128)(2,1)} %collective-permute-done.2, ...), kind=kLoop, calls=%fused_computation | loop fusion | flops 59136000 | bytes 22400000 | tf_op jit(solution)/shard_map/concatenate | solution.py:20
  378.2 29.0 %multiply_add_fusion = f32[8,32,11200]{2,0,1:T(8,128)} fusion(bf16[8,32,11200]{2,0,1:T(8,128)(2,1)S(1)} %bitcast.29, bf16[10,33,11200]{2,0,1:T(8,128)(2,1)} %get-tuple-element.11, bf16[1,32,11200]{2,0,1:T(2,128)(2,1)S(1)} %copy-done.1, bf16[10,33,11200]{2,0,1:T(8,128)(2,1)} %get-tuple-element.10, bf16[1,32,11200]{2,0,1:T(2,128)(2,1)S(1)} %copy.36, ...), kind=kLoop, calls=%fused_computation.2 | loop fusion | flops 94617600 | bytes 53491200 | tf_op jit(solution)/shard_map/add | solution.py:50
  407.1 5.2 %fusion = bf16[8,32,5600]{2,0,1:T(8,128)(2,1)S(1)} fusion(f32[8,32,11200]{2,0,1:T(8,128)} %multiply_add_fusion), kind=kLoop, calls=%fused_computation.4 | loop fusion | flops 8601600 | bytes 14336000 | tf_op jit(solution)/shard_map/convert_element_type | solution.py:51
  412.4 2.4 copy.45
  (57 shorter events, 9.6 us)
Async XLA Ops:
  7.2 12.7 %copy-start.6 = (bf16[8,32,2240]{2,1,0:T(8,128)(2,1)S(1)}, bf16[8,32,2240]{2,1,0:T(8,128)(2,1)}, u32[]{:S(2)}) copy-start(bf16[8,32,2240]{2,1,0:T(8,128)(2,1)} %param.8) | copy-start | bytes 3440644
  7.2 236.7 %all-reduce.3.cloned.1.call-start = ((), (), s32[]{:S(2)}) async-start(), calls=%async_computation | async-start | bytes 589824 | tf_op jit(solution)/shard_map/psum | solution.py:32
  9.6 236.9 %collective-permute-start = (bf16[1,32,11200]{2,1,0:T(8,128)(2,1)S(1)}, bf16[1,32,11200]{2,1,0:T(8,128)(2,1)}, u32[]{:S(2)}, u32[]{:S(2)}) collective-permute-start(bf16[1,32,11200]{2,1,0:T(8,128)(2,1)S(1)} %get-tuple-element.14), channel_id=1, source_target_pairs={{0,8},{8,16},{16,24},{24,32},{32,40},{40,48},{48,56},{56,64},{64,7... | collective-permute-start | bytes 2150408 | tf_op jit(solution)/shard_map/ppermute | solution.py:16
  12.2 236.6 %collective-permute-start.1 = (bf16[1,32,11200]{2,1,0:T(8,128)(2,1)}, bf16[1,32,11200]{2,1,0:T(8,128)(2,1)}, u32[]{:S(2)}, u32[]{:S(2)}) collective-permute-start(bf16[1,32,11200]{2,1,0:T(8,128)(2,1)} %get-tuple-element.15), channel_id=1, source_target_pairs={{8,0},{16,8},{24,16},{32,24},{40,32},{48,40},{56,48},{64,56},{72,6... | collective-permute-start | bytes 2150408 | tf_op jit(solution)/shard_map/ppermute | solution.py:19
  24.8 6.5 %copy-start.7 = (bf16[3,3,11200]{2,1,0:T(4,128)(2,1)S(1)}, bf16[3,3,11200]{2,1,0:T(4,128)(2,1)}, u32[]{:S(2)}) copy-start(bf16[3,3,11200]{2,1,0:T(4,128)(2,1)} %param.10) | copy-start | bytes 604804
  24.8 7.4 %copy-start.5 = (bf16[8,32,2240]{2,1,0:T(8,128)(2,1)S(1)}, bf16[8,32,2240]{2,1,0:T(8,128)(2,1)}, u32[]{:S(2)}) copy-start(bf16[8,32,2240]{2,1,0:T(8,128)(2,1)} %param.6) | copy-start | bytes 3440644
  31.2 308.8 %all-reduce.5.cloned.1.call-start = ((), (), s32[]{:S(2)}) async-start(), calls=%async_computation.1 | async-start | bytes 2293760 | tf_op jit(solution)/shard_map/psum | solution.py:32
  32.4 11.0 %copy-start.2 = (bf16[8,32,2240]{2,1,0:T(8,128)(2,1)S(1)}, bf16[8,32,2240]{2,1,0:T(8,128)(2,1)}, u32[]{:S(2)}) copy-start(bf16[8,32,2240]{2,1,0:T(8,128)(2,1)} %param.7) | copy-start | bytes 3440644
  43.4 109.0 %copy-start.3 = (bf16[256,70,32]{0,2,1:T(8,128)(2,1)}, bf16[256,70,32]{0,2,1:T(8,128)(2,1)S(1)}, u32[]{:S(2)}) copy-start(bf16[256,70,32]{0,2,1:T(8,128)(2,1)S(1)} %copy.50) | copy-start | bytes 3440644
  144.1 8.3 %copy-start.14 = (bf16[11200]{0:T(1024)(128)(2,1)S(1)}, bf16[11200]{0:T(1024)(128)(2,1)}, u32[]{:S(2)}) copy-start(bf16[11200]{0:T(1024)(128)(2,1)} %param.11) | copy-start | bytes 67204
  248.8 91.3 %copy-start.4 = (bf16[256,70,32]{0,2,1:T(8,128)(2,1)S(1)}, bf16[256,70,32]{0,2,1:T(8,128)(2,1)}, u32[]{:S(2)}) copy-start(bf16[256,70,32]{0,2,1:T(8,128)(2,1)} %copy-done.3) | copy-start | bytes 3440644
  251.1 1.1 copy-start
  254.3 101.6 %collective-permute-start.2 = (bf16[10,1,11200]{2,0,1:T(8,128)(2,1)}, bf16[10,1,11200]{2,0,1:T(8,128)(2,1)}, u32[]{:S(2)}, u32[]{:S(2)}) collective-permute-start(bf16[10,1,11200]{2,0,1:T(8,128)(2,1)} %get-tuple-element.12), channel_id=1, source_target_pairs={{0,1},{1,2},{2,3},{3,4},{4,5},{5,6},{6,7},{8,9},{9,10},{10,11},{11... | collective-permute-start | bytes 672008 | tf_op jit(solution)/shard_map/ppermute | solution.py:16
  259.2 96.7 %collective-permute-start.3 = (bf16[10,1,11200]{2,0,1:T(8,128)(2,1)S(1)}, bf16[10,1,11200]{2,0,1:T(8,128)(2,1)}, u32[]{:S(2)}, u32[]{:S(2)}) collective-permute-start(bf16[10,1,11200]{2,0,1:T(8,128)(2,1)S(1)} %get-tuple-element.13), channel_id=1, source_target_pairs={{1,0},{2,1},{3,2},{4,3},{5,4},{6,5},{7,6},{9,8},{10,9},{11,10},{12... | collective-permute-start | bytes 672008 | tf_op jit(solution)/shard_map/ppermute | solution.py:19
  349.5 28.6 %slice-start = ((s8[5767168]{0:T(1024)(128)(4,1)}), s8[1572864]{0:T(1024)(128)(4,1)S(1)}, s32[]{:S(2)}) async-start(s8[5767168]{0:T(1024)(128)(4,1)} %bitcast.28), calls=%async_computation.2 | async-start | bytes 3145728
  355.8 22.2 %slice-start.1 = ((s8[5767168]{0:T(1024)(128)(4,1)}), s8[4194304]{0:T(1024)(128)(4,1)S(1)}, s32[]{:S(2)}) async-start(s8[5767168]{0:T(1024)(128)(4,1)} %bitcast.28), calls=%async_computation.3 | async-start | bytes 8388608
  355.8 22.3 %copy-start.1 = (bf16[1,32,11200]{2,0,1:T(2,128)(2,1)S(1)}, bf16[1,32,11200]{2,0,1:T(2,128)(2,1)}, u32[]{:S(2)}) copy-start(bf16[1,32,11200]{2,0,1:T(2,128)(2,1)} %copy-done) | copy-start | bytes 2150404
  355.8 22.3 %copy-start.8 = (f32[1,1,11200]{2,1,0:T(1,128)S(1)}, f32[1,1,11200]{2,1,0:T(1,128)}, u32[]{:S(2)}) copy-start(f32[1,1,11200]{2,1,0:T(1,128)} %get-tuple-element.19) | copy-start | bytes 134404
  355.8 22.3 %copy-start.9 = (f32[1,1,11200]{2,1,0:T(1,128)S(1)}, f32[1,1,11200]{2,1,0:T(1,128)}, u32[]{:S(2)}) copy-start(f32[1,1,11200]{2,1,0:T(1,128)} %get-tuple-element.20) | copy-start | bytes 134404
  355.8 22.3 %copy-start.10 = (f32[1,1,11200]{2,1,0:T(1,128)S(1)}, f32[1,1,11200]{2,1,0:T(1,128)}, u32[]{:S(2)}) copy-start(f32[1,1,11200]{2,1,0:T(1,128)} %get-tuple-element.21) | copy-start | bytes 134404
  355.8 22.3 %copy-start.11 = (f32[1,1,11200]{2,1,0:T(1,128)S(1)}, f32[1,1,11200]{2,1,0:T(1,128)}, u32[]{:S(2)}) copy-start(f32[1,1,11200]{2,1,0:T(1,128)} %get-tuple-element.22) | copy-start | bytes 134404
  355.9 22.3 %copy-start.12 = (f32[1,1,11200]{2,1,0:T(1,128)S(1)}, f32[1,1,11200]{2,1,0:T(1,128)}, u32[]{:S(2)}) copy-start(f32[1,1,11200]{2,1,0:T(1,128)} %get-tuple-element.23) | copy-start | bytes 134404
  355.9 22.3 %copy-start.13 = (f32[1,1,11200]{2,1,0:T(1,128)S(1)}, f32[1,1,11200]{2,1,0:T(1,128)}, u32[]{:S(2)}) copy-start(f32[1,1,11200]{2,1,0:T(1,128)} %get-tuple-element.24) | copy-start | bytes 134404
Sparse Core Ops, SparseCore 0:
  31.4 212.4 all-reduce.2
  247.3 92.7 all-reduce.4
